TPU v7x, 128 devices: a whole 4x4x4 slice. The times are simulated.
128 devices in a mesh: rows: 32 (over x, y, core), feat: 4 (over z).
Axes of the slice: x: 4, y: 4, z: 4, core: 2. Of those that a mesh axis runs over, the one named last changes fastest.
Arguments:
- design: bfloat16 [8192, 65536], P('rows', 'feat')
- labels: int32 [8192], P('rows'), may hold values from -1 to 1, as said below
- start_position: float32 [16, 65536], P(None, 'feat')
- momenta: float32 [8, 4, 65536], P(None, None, 'feat'), may hold values from -6 to 6
- lag_offsets: int32 [8], replicated, may hold values from 0 to 2, as said below
- accept_bits: int32 [2, 16], replicated, may hold values 0 or 1
- step_sizes: float32 [8], replicated, may hold values from 0.1 to 0.3
Outputs:
- final_position: float32 [16, 65536], P(None, 'feat')
- final_momentum: float32 [16, 65536], P(None, 'feat')
- log_likelihood: float32 [2, 16], replicated
- distance: float32 [2, 8], replicated
Inputs may be any that keep to these rules, and one draw needn't show every extreme that they name: `labels`: each entry is -1 or 1. `lag_offsets`: some pair has lag 0 and some pair has lag 2.
All inputs are finite; a program needn't handle non-finite values.
Results may differ from a plain program's by a relative error of at most 0.00043.
Values may be sent and summed in bfloat16 or wider, within the bound.
No kernel may reach another device: no remote copies, remote signals or barrier semaphores. Data moves between devices by JAX's collectives and lax.ppermute only.
A program may use at most 64 MiB of HBM per device.

v0:
```python
import jax
import jax.numpy as jnp
from jax import lax
from jax.sharding import PartitionSpec as P

FEATURES = 65536
TRANS = 2
LEAP = 5


def on_device(design, labels, start_position, momenta, lag_offsets, accept_bits, step_sizes):
    rows_dev, feat_dev = design.shape
    row_count = lax.axis_size("rows")
    slice_width = feat_dev // row_count
    row_index = lax.axis_index("rows")
    label_signs = labels.astype(jnp.float32)
    chain_steps = jnp.repeat(step_sizes, 2)[:, None]
    position = start_position

    def gradient_at(coefficients):
        rounded = coefficients.astype(jnp.bfloat16)
        partial_margins = lax.dot_general(
            rounded, design, (((1,), (1,)), ((), ())), preferred_element_type=jnp.float32
        )
        margins = lax.psum(partial_margins, "feat")
        weights = (label_signs * jax.nn.sigmoid(-label_signs * margins)).astype(jnp.bfloat16)
        row_terms = jnp.dot(weights, design, preferred_element_type=jnp.float32)
        summed = lax.psum(row_terms, "rows")
        return (margins, summed - coefficients)

    margins, gradient = gradient_at(position)
    bank_slots = jnp.arange(momenta.shape[1])
    likes = []
    distances = []
    momentum = position
    for transition in range(TRANS):
        chosen = bank_slots[None, :] == (transition + lag_offsets)[:, None]
        leader = jnp.sum(jnp.where(chosen[:, :, None], momenta, 0.0), axis=1)
        trailer = momenta[:, transition, :]
        momentum = jnp.stack([leader, trailer], axis=1).reshape(
            2 * leader.shape[0], leader.shape[1]
        )
        momentum = momentum + 0.5 * chain_steps * gradient
        proposal = position
        new_gradient = gradient
        for leap_index in range(LEAP):
            proposal = proposal + chain_steps * momentum
            margins, new_gradient = gradient_at(proposal)
            if leap_index + 1 < LEAP:
                momentum = momentum + chain_steps * new_gradient
            else:
                momentum = momentum + 0.5 * chain_steps * new_gradient
        keep = (accept_bits[transition] == 1)[:, None]
        position = jnp.where(keep, proposal, position)
        gradient = jnp.where(keep, new_gradient, gradient)
        separation = position[0::2] - position[1::2]
        separation = lax.dynamic_slice_in_dim(separation, row_index * slice_width, slice_width, 1)
        square_terms = jnp.sum(separation * separation, axis=1)
        like_terms = jnp.sum(jax.nn.log_sigmoid(label_signs * margins), axis=1)
        like_total = lax.psum(like_terms, "rows")
        square_total = lax.psum(square_terms, ("rows", "feat"))
        likes.append(like_total / (rows_dev * row_count))
        distances.append(jnp.sqrt(square_total / FEATURES + 1e-06))
    return (position, momentum, jnp.stack(likes), jnp.stack(distances))


def solution(mesh):
    return jax.shard_map(
        on_device,
        mesh=mesh,
        in_specs=(
            P("rows", "feat"),
            P("rows"),
            P(None, "feat"),
            P(None, None, "feat"),
            P(),
            P(),
            P(),
        ),
        out_specs=(P(None, "feat"), P(None, "feat"), P(), P()),
        check_vma=False,
    )
```

profile of v0, /device:TPU:1, one launch (start us, length us, event | category | flops | bytes accessed | tf_op | source)
XLA Modules:
  0.0 1513.8 jit_solution(12732637879425066755)
XLA Ops:
  8.6 6.0 fusion.21
  14.6 15.4 %psum.182 = f32[16,256]{1,0:T(8,128)S(1)} all-reduce(f32[16,256]{1,0:T(8,128)S(1)} %fusion.21), channel_id=1, replica_groups=mesh['rows'=32,'feat'=4] {'feat'}, use_global_device_ids=true, to_apply=%region_1.0 | all-reduce | flops 4096 | bytes 32768 | tf_op jit(solution)/shard_map/psum | solution.py:25
  29.9 5.6 fusion.30
  36.1 4.1 fusion.85
  40.6 5.5 select_reduce_fusion
  46.3 1.8 copy.12
  48.1 1.9 reshape.80
  50.1 93.7 %all-reduce.14.cloned.1.call-done = f32[16,16384]{1,0:T(8,128)} async-done(((f32[16,16384]{1,0:T(8,128)}), f32[16,16384]{1,0:T(8,128)}) %all-reduce.14.cloned.1.call-update) | async-done | bytes 1048592 | tf_op jit(solution)/shard_map/psum | solution.py:28
  145.1 6.0 fusion.19
  151.1 13.3 psum.184
  164.4 5.6 fusion.31
  170.3 105.9 %all-reduce.16.cloned.1.call-done = f32[16,16384]{1,0:T(8,128)} async-done(((f32[16,16384]{1,0:T(8,128)}), f32[16,16384]{1,0:T(8,128)}) %all-reduce.16.cloned.1.call-update) | async-done | bytes 1048592 | tf_op jit(solution)/shard_map/psum | solution.py:28
  276.2 1.9 multiply_add_fusion.16
  278.1 5.6 fusion.17
  283.7 13.3 psum.186
  297.1 5.6 fusion.32
  302.7 106.1 %all-reduce.18.cloned.1.call-done = f32[16,16384]{1,0:T(8,128)} async-done(((f32[16,16384]{1,0:T(8,128)}), f32[16,16384]{1,0:T(8,128)}) %all-reduce.18.cloned.1.call-update) | async-done | bytes 1048592 | tf_op jit(solution)/shard_map/psum | solution.py:28
  408.8 2.3 multiply_add_fusion.15
  412.0 5.6 fusion.15
  417.7 13.5 psum.188
  431.2 5.6 fusion.33
  436.8 106.1 %all-reduce.20.cloned.1.call-done = f32[16,16384]{1,0:T(8,128)} async-done(((f32[16,16384]{1,0:T(8,128)}), f32[16,16384]{1,0:T(8,128)}) %all-reduce.20.cloned.1.call-update) | async-done | bytes 1048592 | tf_op jit(solution)/shard_map/psum | solution.py:28
  542.9 6.0 fusion.1
  548.9 13.5 psum.190
  562.3 5.6 fusion.34
  569.3 104.7 %all-reduce.22.cloned.1.call-done = f32[16,16384]{1,0:T(8,128)} async-done(((f32[16,16384]{1,0:T(8,128)}), f32[16,16384]{1,0:T(8,128)}) %all-reduce.22.cloned.1.call-update) | async-done | bytes 1048592 | tf_op jit(solution)/shard_map/psum | solution.py:28
  674.1 2.4 broadcast_select_fusion
  677.5 5.6 fusion.13
  683.1 13.3 psum.192
  696.5 5.7 fusion.35
  703.5 1.8 copy.14
  705.3 2.9 reshape.81
  708.2 100.1 %all-reduce.24.cloned.1.call-done = f32[16,16384]{1,0:T(8,128)} async-done(((f32[16,16384]{1,0:T(8,128)}), f32[16,16384]{1,0:T(8,128)}) %all-reduce.24.cloned.1.call-update) | async-done | bytes 1048592 | tf_op jit(solution)/shard_map/psum | solution.py:28
  808.4 1.8 multiply_add_fusion.10
  811.1 5.6 fusion.11
  816.8 13.5 psum.194
  830.3 5.6 fusion.36
  836.3 105.6 %all-reduce.26.cloned.1.call-done = f32[16,16384]{1,0:T(8,128)} async-done(((f32[16,16384]{1,0:T(8,128)}), f32[16,16384]{1,0:T(8,128)}) %all-reduce.26.cloned.1.call-update) | async-done | bytes 1048592 | tf_op jit(solution)/shard_map/psum | solution.py:28
  941.9 1.5 multiply_add_fusion.7
  943.5 5.6 fusion.9
  949.1 13.3 psum.196
  962.4 5.6 fusion.37
  968.1 106.1 %all-reduce.28.cloned.1.call-done = f32[16,16384]{1,0:T(8,128)} async-done(((f32[16,16384]{1,0:T(8,128)}), f32[16,16384]{1,0:T(8,128)}) %all-reduce.28.cloned.1.call-update) | async-done | bytes 1048592 | tf_op jit(solution)/shard_map/psum | solution.py:28
  1074.2 2.2 multiply_add_fusion.6
  1076.4 6.0 fusion.7
  1082.4 13.3 psum.198
  1095.7 5.6 fusion.38
  1101.4 106.0 %all-reduce.30.cloned.1.call-done = f32[16,16384]{1,0:T(8,128)} async-done(((f32[16,16384]{1,0:T(8,128)}), f32[16,16384]{1,0:T(8,128)}) %all-reduce.30.cloned.1.call-update) | async-done | bytes 1048592 | tf_op jit(solution)/shard_map/psum | solution.py:28
  1207.4 1.9 multiply_add_fusion.3
  1209.3 5.6 fusion.5
  1214.9 13.3 psum.200
  1228.2 5.6 fusion.39
  1234.0 2.5 slice.29
  1236.5 2.4 slice.28
  1239.8 100.2 %all-reduce.32.cloned.1.call-done = f32[16,16384]{1,0:T(8,128)} async-done(((f32[16,16384]{1,0:T(8,128)}), f32[16,16384]{1,0:T(8,128)}) %all-reduce.32.cloned.1.call-update) | async-done | bytes 1048592 | tf_op jit(solution)/shard_map/psum | solution.py:28
  1340.0 3.3 broadcast_select_fusion.1
  1344.2 5.7 fusion.3
  1350.0 13.5 psum.202
  1363.4 5.6 fusion.40
  1369.1 2.5 slice.31
  1371.6 2.4 slice.30
  1374.0 66.7 %all-reduce.1 = (f32[16]{0:T(128)S(1)}, f32[16]{0:T(128)S(1)}) all-reduce(f32[16]{0:T(128)S(1)} %neg.85, f32[16]{0:T(128)S(1)} %neg.82), channel_id=1, replica_groups=mesh['rows'=32,'feat'=4] {'rows'}, use_global_device_ids=true, to_apply=%region_27.28 | all-reduce | flops 32 | bytes 256 | tf_op jit(solution)/shard_map/psum | solution.py:60
  1442.2 61.9 %all-reduce = (f32[8]{0:T(128)S(1)}, f32[8]{0:T(128)S(1)}) all-reduce(f32[8]{0:T(128)S(1)} %fusion.27, f32[8]{0:T(128)S(1)} %fusion.29), channel_id=1, replica_groups=mesh['rows'=32,'feat'=4] {'rows','feat'}, use_global_device_ids=true, to_apply=%region_31.32 | all-reduce | flops 16 | bytes 128 | tf_op jit(solution)/shard_map/psum | solution.py:61
  1504.7 2.4 multiply_add_fusion
  (83 shorter events, 14.8 us)
Async XLA Ops:
  7.2 136.6 %all-reduce.14.cloned.1.call-start = ((), (), s32[]{:S(2)}) async-start(), calls=%async_computation | async-start | bytes 2097152 | tf_op jit(solution)/shard_map/psum | solution.py:28
  14.6 25.9 %copy-start.17 = (s32[8]{0:T(128)S(1)}, s32[8]{0:T(128)}, u32[]{:S(2)}) copy-start(s32[8]{0:T(128)} %param.11) | copy-start | bytes 100
  29.9 16.2 %copy-start.16 = (f32[8]{0:T(128)S(1)}, f32[8]{0:T(128)}, u32[]{:S(2)}) copy-start(f32[8]{0:T(128)} %param.13) | copy-start | bytes 100
  35.5 108.2 %copy-start = (f32[16,16384]{1,0:T(8,128)S(1)}, f32[16,16384]{1,0:T(8,128)}, u32[]{:S(2)}) copy-start(f32[16,16384]{1,0:T(8,128)} %param.9) | copy-start | bytes 3145732
  35.5 240.6 %all-reduce.16.cloned.1.call-start = ((), (), s32[]{:S(2)}) async-start(), calls=%async_computation.1 | async-start | bytes 2097152 | tf_op jit(solution)/shard_map/psum | solution.py:28
  50.1 119.9 %copy-start.4 = (f32[16,16384]{1,0:T(8,128)}, f32[16,16384]{1,0:T(8,128)S(1)}, u32[]{:S(2)}) copy-start(f32[16,16384]{1,0:T(8,128)S(1)} %reshape.80) | copy-start | bytes 3145732
  145.1 263.7 %copy-start.1 = (f32[16,16384]{1,0:T(8,128)}, f32[16,16384]{1,0:T(8,128)S(1)}, u32[]{:S(2)}) copy-start(f32[16,16384]{1,0:T(8,128)S(1)} %sub.39) | copy-start | bytes 3145732
  170.0 238.8 %all-reduce.18.cloned.1.call-start = ((), (), s32[]{:S(2)}) async-start(), calls=%async_computation.2 | async-start | bytes 2097152 | tf_op jit(solution)/shard_map/psum | solution.py:28
  302.7 240.2 %all-reduce.20.cloned.1.call-start = ((), (), s32[]{:S(2)}) async-start(), calls=%async_computation.3 | async-start | bytes 2097152 | tf_op jit(solution)/shard_map/psum | solution.py:28
  411.1 1.0 copy-start.7
  417.7 125.2 %copy-start.8 = (f32[16,16384]{1,0:T(8,128)S(1)}, f32[16,16384]{1,0:T(8,128)}, u32[]{:S(2)}) copy-start(f32[16,16384]{1,0:T(8,128)} %copy-done.7) | copy-start | bytes 3145732
  436.7 237.3 %all-reduce.22.cloned.1.call-start = ((), (), s32[]{:S(2)}) async-start(), calls=%async_computation.4 | async-start | bytes 2097152 | tf_op jit(solution)/shard_map/psum | solution.py:28
  548.9 19.3 %copy-start.14 = (f32[8,1,16384]{2,1,0:T(1,128)S(1)}, f32[8,1,16384]{2,1,0:T(1,128)}, u32[]{:S(2)}) copy-start(f32[8,1,16384]{2,1,0:T(1,128)} %get-tuple-element.16) | copy-start | bytes 1572868
  548.9 20.5 %copy-start.15 = (s32[2,16]{1,0:T(2,128)S(1)}, s32[2,16]{1,0:T(2,128)}, u32[]{:S(2)}) copy-start(s32[2,16]{1,0:T(2,128)} %param.12) | copy-start | bytes 388
  567.9 240.4 %all-reduce.24.cloned.1.call-start = ((), (), s32[]{:S(2)}) async-start(), calls=%async_computation.5 | async-start | bytes 2097152 | tf_op jit(solution)/shard_map/psum | solution.py:28
  676.5 1.0 copy-start.11
  696.5 111.9 %copy-start.2 = (f32[16,16384]{1,0:T(8,128)S(1)}, f32[16,16384]{1,0:T(8,128)}, u32[]{:S(2)}) copy-start(f32[16,16384]{1,0:T(8,128)} %copy-done.1) | copy-start | bytes 3145732
  696.5 111.9 %copy-start.12 = (f32[16,16384]{1,0:T(8,128)S(1)}, f32[16,16384]{1,0:T(8,128)}, u32[]{:S(2)}) copy-start(f32[16,16384]{1,0:T(8,128)} %copy-done.11) | copy-start | bytes 3145732
  702.2 239.7 %all-reduce.26.cloned.1.call-start = ((), (), s32[]{:S(2)}) async-start(), calls=%async_computation.6 | async-start | bytes 2097152 | tf_op jit(solution)/shard_map/psum | solution.py:28
  810.2 1.0 copy-start.5
  816.8 125.1 %copy-start.6 = (f32[16,16384]{1,0:T(8,128)S(1)}, f32[16,16384]{1,0:T(8,128)}, u32[]{:S(2)}) copy-start(f32[16,16384]{1,0:T(8,128)} %copy-done.5) | copy-start | bytes 3145732
  835.8 238.3 %all-reduce.28.cloned.1.call-start = ((), (), s32[]{:S(2)}) async-start(), calls=%async_computation.7 | async-start | bytes 2097152 | tf_op jit(solution)/shard_map/psum | solution.py:28
  968.0 239.4 %all-reduce.30.cloned.1.call-start = ((), (), s32[]{:S(2)}) async-start(), calls=%async_computation.8 | async-start | bytes 2097152 | tf_op jit(solution)/shard_map/psum | solution.py:28
  1076.4 25.0 %copy-start.3 = (f32[16,16384]{1,0:T(8,128)}, f32[16,16384]{1,0:T(8,128)S(1)}, u32[]{:S(2)}) copy-start(f32[16,16384]{1,0:T(8,128)S(1)} %multiply_add_fusion.6) | copy-start | bytes 3145732
  1101.3 238.6 %all-reduce.32.cloned.1.call-start = ((), (), s32[]{:S(2)}) async-start(), calls=%async_computation.9 | async-start | bytes 2097152 | tf_op jit(solution)/shard_map/psum | solution.py:28
  1233.8 270.8 %all-reduce.34.cloned.1.call-start = ((), (), s32[]{:S(2)}) async-start(), calls=%async_computation.10 | async-start | bytes 2097152 | tf_op jit(solution)/shard_map/psum | solution.py:28
  1343.2 1.0 copy-start.9
  1344.2 24.9 %copy-start.13 = (f32[16,16384]{1,0:T(8,128)S(1)}, f32[16,16384]{1,0:T(8,128)}, u32[]{:S(2)}) copy-start(f32[16,16384]{1,0:T(8,128)} %get-tuple-element.12) | copy-start | bytes 3145732
  1349.9 154.7 %copy-start.10 = (f32[16,16384]{1,0:T(8,128)S(1)}, f32[16,16384]{1,0:T(8,128)}, u32[]{:S(2)}) copy-start(f32[16,16384]{1,0:T(8,128)} %copy-done.9) | copy-start | bytes 3145732
Sparse Core Ops, SparseCore 0:
  35.7 108.0 all-reduce.13
  170.2 105.9 all-reduce.15
  302.8 105.9 all-reduce.17
  436.9 105.9 all-reduce.19
  568.0 105.9 all-reduce.21
  702.3 105.9 all-reduce.23
  836.0 105.9 all-reduce.25
  968.1 105.9 all-reduce.27
  1101.4 105.9 all-reduce.29
  1233.9 105.9 all-reduce.31
  1374.2 106.0 all-reduce.33
where the time goes:
time: 1520 us; the launch traced here: 1510 us
  waiting for transfers between devices  1030 us (68%)
  blocking collectives  278 us (18%)
  matrix products  125 us (8%)
  other arithmetic  32.4 us (2%)
  local copies, waits for them, and re-layouts  27.8 us (2%)
    psum x11, waiting for transfers between devices, gradient_at(): summed = lax.psum(row_terms, 'rows')  1030 us
    psum x11, blocking collectives, gradient_at(): margins = lax.psum(partial_margins, 'feat')  149 us
    psum x1, blocking collectives, on_device(): like_total = lax.psum(like_terms, 'rows')  66.7 us
    dot_general x11, matrix products, gradient_at(): lax.dot_general(rounded, design, (((1,), (1,)), ((), ())), preferred_elem...  63.6 us
    psum x1, blocking collectives, on_device(): square_total = lax.psum(square_terms, ('rows', 'feat'))  61.9 us
    dot_general x11, matrix products, gradient_at(): row_terms = jnp.dot(weights, design, preferred_element_type=jnp.float32)  61.3 us
  transfers between devices with their start and end apart: 11, of which 10 were waited for; matrix products, arithmetic and copies ran while one was open for 2% of the time, Pallas kernels for 0%

commit v1 on v0

v1 whole, which is shorter than its diff:
```python
import jax
import jax.numpy as jnp
from jax import lax
from jax.experimental import pallas as pl
from jax.experimental.pallas import tpu as pltpu
from jax.sharding import PartitionSpec as P

FEATURES = 65536
TRANS = 2
LEAP = 5
CHAINS = 16
EXTRA = 128
CHUNKS = 8

F32 = jnp.float32
BF16 = jnp.bfloat16
VMEM = pl.BlockSpec(memory_space=pltpu.VMEM)
ANY = pl.BlockSpec(memory_space=pl.ANY)


def params(mib):
    return pltpu.CompilerParams(vmem_limit_bytes=mib * 1024 * 1024)


def lane_iota():
    return lax.broadcasted_iota(jnp.int32, (CHAINS, EXTRA), 1)


def split3(column, first_lane):
    lanes = lane_iota() - first_lane
    high = column.astype(BF16).astype(F32)
    middle = (column - high).astype(BF16).astype(F32)
    low = column - high - middle
    zero = jnp.zeros((CHAINS, EXTRA), F32)
    out = jnp.where(lanes == 0, high, zero)
    out = jnp.where(lanes == 1, middle, out)
    return jnp.where(lanes == 2, low, out)


def margins_kernel(coefficients, design, extended):
    rows, width = design.shape
    blocked = coefficients.ndim == 3
    step = width // CHUNKS
    out_width = rows + (EXTRA if extended else 0)

    def body(coef_ref, design_ref, margins_ref, held_ref, sems):
        copies = [
            pltpu.make_async_copy(
                design_ref.at[:, pl.ds(i * step, step)],
                held_ref.at[:, pl.ds(i * step, step)],
                sems.at[i],
            )
            for i in range(CHUNKS)
        ]
        for copy in copies:
            copy.start()
        total = jnp.zeros((CHAINS, rows), F32)
        if extended:
            side = jnp.zeros((CHAINS, EXTRA), F32)
            block = coef_ref.shape[2] - EXTRA
            for b in range(coef_ref.shape[0]):
                side = side + coef_ref[b, :, block:].astype(F32)
            margins_ref[:, rows:] = side
        for i in range(CHUNKS):
            copies[i].wait()
            if blocked:
                block = coef_ref.shape[2] - (EXTRA if extended else 0)
                for j in range(step // block):
                    at = i * step + j * block
                    total = total + lax.dot_general(
                        coef_ref[at // block, :, :block],
                        held_ref[:, at : at + block],
                        (((1,), (1,)), ((), ())),
                        preferred_element_type=F32,
                    )
            else:
                total = total + lax.dot_general(
                    coef_ref[:, i * step : (i + 1) * step].astype(BF16),
                    held_ref[:, i * step : (i + 1) * step],
                    (((1,), (1,)), ((), ())),
                    preferred_element_type=F32,
                )
        margins_ref[:, :rows] = total

    return pl.pallas_call(
        body,
        in_specs=[VMEM, ANY],
        out_specs=[VMEM, VMEM],
        out_shape=[
            jax.ShapeDtypeStruct((CHAINS, out_width), F32),
            jax.ShapeDtypeStruct(design.shape, design.dtype),
        ],
        scratch_shapes=[pltpu.SemaphoreType.DMA((CHUNKS,))],
        compiler_params=params(16),
        cost_estimate=pl.CostEstimate(
            flops=2 * CHAINS * rows * width, bytes_accessed=2 * rows * width, transcendentals=0
        ),
        name="margins",
    )(coefficients, design)


def terms_kernel(partials, signs, held, blocks, likes, earlier_likes):
    rows, width = held.shape
    block = width // blocks
    extended = earlier_likes is not None
    total_width = partials[0].shape[1]
    out_block = block + (EXTRA if extended else 0)

    def body(*refs):
        own, one, two, three, sign_ref, held_ref = refs[:6]
        rest = list(refs[6:])
        earlier_ref = rest.pop(0) if extended else None
        out_ref = rest.pop(0)
        total = (own[...] + two[...]) + (one[...] + three[...])
        sign = sign_ref[...]
        signed = sign * total[:, :rows]
        weights = (sign * jax.nn.sigmoid(-signed)).astype(BF16)
        if likes:
            terms = jnp.minimum(signed, 0.0) - jnp.log1p(jnp.exp(-jnp.abs(signed)))
            like = jnp.sum(terms, axis=1, keepdims=True)
            if extended:
                side = split3(earlier_ref[...][:, :1], 0) + split3(like, 3)
                side = side.astype(BF16)
                for b in range(blocks):
                    out_ref[b, :, block:] = side
                rest[0][...] = total[:, rows:]
            else:
                rest[0][...] = jnp.broadcast_to(like, (CHAINS, EXTRA))
        group = 4
        for b in range(0, blocks, group):
            terms = lax.dot_general(
                weights,
                held_ref[:, b * block : (b + group) * block],
                (((1,), (0,)), ((), ())),
                preferred_element_type=F32,
            ).astype(BF16)
            for j in range(group):
                out_ref[b + j, :, :block] = terms[:, j * block : (j + 1) * block]

    args = list(partials) + [signs, held] + ([earlier_likes] if extended else [])
    outs = [jax.ShapeDtypeStruct((blocks, CHAINS, out_block), BF16)]
    if likes:
        outs.append(jax.ShapeDtypeStruct((CHAINS, EXTRA), F32))
    del total_width
    return pl.pallas_call(
        body,
        in_specs=[VMEM] * len(args),
        out_specs=[VMEM] * len(outs),
        out_shape=outs,
        compiler_params=params(16),
        cost_estimate=pl.CostEstimate(
            flops=2 * CHAINS * rows * width, bytes_accessed=2 * rows * width, transcendentals=0
        ),
        name="terms",
    )(*args)


def summed(ref, block):
    parts = [ref[b, :, :block].astype(F32) for b in range(ref.shape[0])]
    while len(parts) > 1:
        parts = [parts[i] + parts[i + 1] for i in range(0, len(parts), 2)]
    return parts[0]


def square_gap(position):
    gap = position - pltpu.roll(position, CHAINS - 1, 0)
    return jnp.sum(gap * gap, axis=1, keepdims=True)


def step_kernel(mode, arrived, state, blocks):
    names = list(state)
    block = 512
    wide = mode == "before_last"
    out_block = block + (EXTRA if wide else 0)
    outs = {"send": ((blocks, CHAINS, out_block), BF16)}
    slice_names = {
        "first": ["q", "p", "g0"],
        "mid": ["q", "p"],
        "turn": ["q", "p", "pos", "gap"],
        "before_last": ["q", "p"],
        "last": [],
    }[mode]
    for name in slice_names:
        outs[name] = ((CHAINS, EXTRA if name == "gap" else block), F32)
    if mode == "before_last":
        outs["ends"] = ((blocks, 2 * CHAINS, block), F32)
    if mode == "last":
        outs["likes"] = ((CHAINS, EXTRA), F32)

    def body(*refs):
        arrived_ref = refs[0]
        vals = {n: r[...] for n, r in zip(names, refs[1 : 1 + len(names)])}
        out = dict(zip(outs, refs[1 + len(names) :]))
        g = summed(arrived_ref, block)
        if mode == "last":
            side = jnp.zeros((CHAINS, EXTRA), F32)
            for b in range(blocks):
                side = side + arrived_ref[b, :, block:].astype(F32)
            out["likes"][...] = side
            send = g.astype(BF16)
            for b in range(blocks):
                out["send"][b] = send
            return
        h = vals["h"]
        if mode == "first":
            p = vals["mom"] + 0.5 * h * (g - vals["q"])
            q = vals["q"] + h * p
            out["g0"][...] = g
        elif mode == "turn":
            keep = vals["keep"] != 0.0
            pos = jnp.where(keep, vals["q"], vals["q0"])
            gradient = jnp.where(keep, g - vals["q"], vals["g0"] - vals["q0"])
            p = vals["mom"] + 0.5 * h * gradient
            q = pos + h * p
            out["pos"][...] = pos
            out["gap"][...] = jnp.broadcast_to(square_gap(pos), (CHAINS, EXTRA))
        else:
            p = vals["p"] + h * (g - vals["q"])
            q = vals["q"] + h * p
        out["q"][...] = q
        out["p"][...] = p
        send = q.astype(BF16)
        for b in range(blocks):
            out["send"][b, :, :block] = send
        if mode == "before_last":
            keep = vals["keep"] != 0.0
            pos = jnp.where(keep, q, vals["pos"])
            side = split3(vals["gap"][:, :1], 0) + split3(square_gap(pos), 3)
            side = side.astype(BF16)
            base = p - 0.5 * h * q
            for b in range(blocks):
                out["send"][b, :, block:] = side
                out["ends"][b, :CHAINS] = pos
                out["ends"][b, CHAINS:] = base

    result = pl.pallas_call(
        body,
        in_specs=[VMEM] * (1 + len(names)),
        out_specs=[VMEM] * len(outs),
        out_shape=[jax.ShapeDtypeStruct(*v) for v in outs.values()],
        compiler_params=params(16),
        name="step_" + mode,
    )(arrived, *state.values())
    return dict(zip(outs, result))


def finish_kernel(ends, arrived, half_step):
    blocks, _, block = arrived.shape
    group = 8

    def body(ends_ref, arrived_ref, half_ref, pos_ref, mom_ref):
        for b in range(group):
            cols = pl.ds(b * block, block)
            pos_ref[:, cols] = ends_ref[b, :CHAINS]
            mom_ref[:, cols] = ends_ref[b, CHAINS:] + half_ref[...] * arrived_ref[b].astype(F32)

    shape = jax.ShapeDtypeStruct((CHAINS, blocks * block), F32)
    out_spec = pl.BlockSpec((CHAINS, group * block), lambda i: (0, i))
    return pl.pallas_call(
        body,
        grid=(blocks // group,),
        in_specs=[
            pl.BlockSpec((group, 2 * CHAINS, block), lambda i: (i, 0, 0)),
            pl.BlockSpec((group, CHAINS, block), lambda i: (i, 0, 0)),
            pl.BlockSpec((CHAINS, block), lambda i: (0, 0)),
        ],
        out_specs=[out_spec, out_spec],
        out_shape=[shape, shape],
        compiler_params=params(16),
        name="finish",
    )(ends, arrived, half_step)


def on_device(design, labels, start_position, momenta, lag_offsets, accept_bits, step_sizes):
    rows, width = design.shape
    blocks = lax.axis_size("rows")
    ring = lax.axis_size("feat")
    block = width // blocks
    at = lax.axis_index("rows") * block
    signs = labels.astype(F32)[None, :]

    chain_steps = jnp.repeat(step_sizes, 2)[:, None]
    h = jnp.broadcast_to(chain_steps, (CHAINS, block))
    keeps = [
        jnp.broadcast_to(accept_bits[s].astype(F32)[:, None], (CHAINS, block)) for s in range(TRANS)
    ]
    start = lax.dynamic_slice_in_dim(start_position, at, block, 1)
    draws = lax.dynamic_slice_in_dim(momenta, at, block, 2)
    slots = jnp.arange(momenta.shape[1])
    moms = []
    for s in range(TRANS):
        chosen = slots[None, :] == (s + lag_offsets)[:, None]
        leader = jnp.sum(jnp.where(chosen[:, :, None], draws, 0.0), axis=1)
        moms.append(jnp.stack([leader, draws[:, s]], axis=1).reshape(CHAINS, block))

    def exchange(blocked):
        return lax.all_to_all(blocked, "rows", 0, 0)

    def around(margins):
        return [margins] + [
            lax.ppermute(margins, "feat", [(i, (i + k) % ring) for i in range(ring)])
            for k in range(1, ring)
        ]

    def terms_at(coefficients, likes=False, earlier=None):
        margins, held = margins_kernel(coefficients, design, earlier is not None)
        return terms_kernel(around(margins), signs, held, blocks, likes, earlier)

    (out,) = terms_at(start_position)
    now = step_kernel("first", exchange(out), {"q": start, "mom": moms[0], "h": h}, blocks)
    g0 = now["g0"]
    for _ in range(LEAP - 1):
        (out,) = terms_at(exchange(now["send"]))
        now = step_kernel("mid", exchange(out), {"q": now["q"], "p": now["p"], "h": h}, blocks)
    out, like = terms_at(exchange(now["send"]), likes=True)
    now = step_kernel(
        "turn",
        exchange(out),
        {"q": now["q"], "q0": start, "g0": g0, "mom": moms[1], "h": h, "keep": keeps[0]},
        blocks,
    )
    position, gap = now["pos"], now["gap"]
    for leap in range(LEAP - 1):
        (out,) = terms_at(exchange(now["send"]))
        state = {"q": now["q"], "p": now["p"], "h": h}
        if leap + 2 < LEAP:
            now = step_kernel("mid", exchange(out), state, blocks)
        else:
            state.update(pos=position, gap=gap, keep=keeps[1])
            now = step_kernel("before_last", exchange(out), state, blocks)
    gathered = exchange(now["send"])
    ends, gathered = lax.optimization_barrier((now["ends"], gathered))
    ends = exchange(ends)
    out, gaps = terms_at(gathered, likes=True, earlier=like)
    now = step_kernel("last", exchange(out), {}, blocks)
    final_position, final_momentum = finish_kernel(ends, exchange(now["send"]), 0.5 * h)
    likes = now["likes"][:, :6].reshape(CHAINS, 2, 3).sum(2).T
    squares = gaps[0::2, :6].reshape(CHAINS // 2, 2, 3).sum(2).T
    return (
        final_position,
        final_momentum,
        likes / (rows * blocks),
        jnp.sqrt(squares / FEATURES + 1e-06),
    )


def solution(mesh):
    return jax.shard_map(
        on_device,
        mesh=mesh,
        in_specs=(
            P("rows", "feat"),
            P("rows"),
            P(None, "feat"),
            P(None, None, "feat"),
            P(),
            P(),
            P(),
        ),
        out_specs=(P(None, "feat"), P(None, "feat"), P(), P()),
        check_vma=False,
    )
```

time: 1520 us -> 566 us (0.37)
  waiting for transfers between devices: 1030 us -> 72.1 us
  matrix products: 125 us -> 0 us
  Pallas kernels: 0 us -> 82.5 us
  starting transfers between devices: 1.94 us -> 59.7 us
  blocking collectives: 278 us -> 319 us
  other arithmetic: 32.4 us -> 1.31 us
    psum x11 -> x0, waiting for transfers between devices: 1030 us -> none  [gradient_at(): summed = lax.psum(row_terms, 'rows')]
    all_to_all x0 -> x20, blocking collectives: none -> 319 us  [exchange(): return lax.all_to_all(blocked, 'rows', 0, 0)]
    psum x13 -> x0, blocking collectives: 278 us -> none  [the longest x11 149 us: gradient_at(): margins = lax.psum(partial_margins, 'feat')]
    dot_general x22 -> x0, matrix products: 125 us -> none  [the longest x11 63.6 us: gradient_at(): lax.dot_general(rounded, design, (((1,), (1,)), ((), ())), preferred_elem...]
    pallas_call x0 -> x34, Pallas kernels: none -> 82.5 us  [the longest x11 61.1 us: margins_kernel(): pl.pallas_call(body, in_specs=[VMEM, ANY], out_specs=[VMEM, VMEM], out_sh...]
    all_to_all x0 -> x3, waiting for transfers between devices: none -> 48.6 us  [exchange(): return lax.all_to_all(blocked, 'rows', 0, 0)]
    ppermute x0 -> x33, starting transfers between devices: none -> 40.4 us  [around(): lax.ppermute(margins, 'feat', [(i, (i + k) % ring) for i in range(ring)])]
    ppermute x0 -> x33, waiting for transfers between devices: none -> 23.5 us  [around(): lax.ppermute(margins, 'feat', [(i, (i + k) % ring) for i in range(ring)])]
  transfers between devices with their start and end apart: 11 -> 36, of which waited for: 10 -> 35; matrix products, arithmetic and copies ran while one was open for 2% -> 0% of each run, Pallas kernels for 0% -> 0%
where the time goes in v1:
time: 566 us; the launch traced here: 557 us
  blocking collectives  319 us (56%)
  Pallas kernels  82.5 us (15%)
  waiting for transfers between devices  72.1 us (13%)
  starting transfers between devices  59.7 us (11%)
  local copies, waits for them, and re-layouts  21.2 us (4%)
    all_to_all x20, blocking collectives, exchange(): return lax.all_to_all(blocked, 'rows', 0, 0)  319 us
    pallas_call x11, Pallas kernels, margins_kernel(): pl.pallas_call(body, in_specs=[VMEM, ANY], out_specs=[VMEM, VMEM], out_sh...  61.1 us
    all_to_all x3, waiting for transfers between devices, exchange(): return lax.all_to_all(blocked, 'rows', 0, 0)  48.6 us
    ppermute x33, starting transfers between devices, around(): lax.ppermute(margins, 'feat', [(i, (i + k) % ring) for i in range(ring)])  40.4 us
    ppermute x33, waiting for transfers between devices, around(): lax.ppermute(margins, 'feat', [(i, (i + k) % ring) for i in range(ring)])  23.5 us
    unnamed x36, local copies, waits for them, and re-layouts  19.6 us
    all_to_all x3, starting transfers between devices, exchange(): return lax.all_to_all(blocked, 'rows', 0, 0)  19.2 us
    pallas_call x11, Pallas kernels, terms_kernel(): pl.pallas_call(body, in_specs=[VMEM] * len(args), out_specs=[VMEM] * len(...  14.7 us
  transfers between devices with their start and end apart: 36, of which 35 were waited for; matrix products, arithmetic and copies ran while one was open for 0% of the time, Pallas kernels for 0%

profile of v1, /device:TPU:1, one launch (start us, length us, event | category | flops | bytes accessed | tf_op | source)
XLA Modules:
  0.0 557.2 jit_solution(11917336992386360265)
XLA Ops:
  0.7 3.5 copy-done.2
  4.2 1.2 copy-done.8
  5.4 5.6 %margins.11 = (f32[16,256]{1,0:T(8,128)S(1)}, bf16[256,16384]{1,0:T(8,128)(2,1)S(1)}) custom-call(f32[16,16384]{1,0:T(8,128)S(1)} %copy-done.8, bf16[256,16384]{1,0:T(8,128)(2,1)S(1)} %copy-done.2), custom_call_target="tpu_custom_call" | custom-call | flops 134217728 | bytes 8388608 | tf_op jit(solution)/shard_map/margins/pallas_call | solution.py:85
  11.0 3.3 copy-done.5
  14.4 2.5 collective-permute-start
  16.8 3.3 collective-permute-start.1
  21.4 1.4 collective-permute-done.2.refs_3_
  22.9 3.4 copy-done.6
  26.2 2.0 terms.11
  28.2 9.3 %all-to-all-start = ((bf16[32,16,512]{2,1,0:T(8,128)(2,1)}), bf16[32,16,512]{2,1,0:T(8,128)(2,1)S(1)}, u32[]{:S(2)}, u32[]{:S(2)}) async-start(bf16[32,16,512]{2,1,0:T(8,128)(2,1)} %terms.11), calls=%async_computation | async-start | bytes 1048576 | tf_op jit(solution)/shard_map/all_to_all | solution.py:297
  38.7 10.5 %all-to-all-done.refs_0_ = bf16[32,16,512]{2,1,0:T(8,128)(2,1)S(1)} async-done(((bf16[32,16,512]{2,1,0:T(8,128)(2,1)}), bf16[32,16,512]{2,1,0:T(8,128)(2,1)S(1)}, u32[]{:S(2)}, u32[]{:S(2)}) %all-to-all-start) | async-done | bytes 524320 | tf_op jit(solution)/shard_map/all_to_all | solution.py:297
  49.4 15.0 %all_to_all.115.coef_ref = bf16[32,16,512]{2,1,0:T(8,128)(2,1)S(1)} all-to-all(bf16[32,16,512]{2,1,0:T(8,128)(2,1)S(1)} %get-tuple-element.69), channel_id=1, replica_groups=mesh['rows'=32,'feat'=4] {'rows'}, dimensions={0} | all-to-all | bytes 1048576 | tf_op jit(solution)/shard_map/all_to_all | solution.py:297
  64.4 3.4 copy-done.3
  67.8 5.5 margins.12
  73.4 3.1 collective-permute-start.4
  80.3 16.9 %all_to_all.116.refs_0_ = bf16[32,16,512]{2,1,0:T(8,128)(2,1)S(1)} all-to-all(bf16[32,16,512]{2,1,0:T(8,128)(2,1)S(1)} %terms.12), channel_id=1, replica_groups=mesh['rows'=32,'feat'=4] {'rows'}, dimensions={0} | all-to-all | bytes 1048576 | tf_op jit(solution)/shard_map/all_to_all | solution.py:297
  97.3 15.5 %all_to_all.117.coef_ref = bf16[32,16,512]{2,1,0:T(8,128)(2,1)S(1)} all-to-all(bf16[32,16,512]{2,1,0:T(8,128)(2,1)S(1)} %get-tuple-element.74), channel_id=1, replica_groups=mesh['rows'=32,'feat'=4] {'rows'}, dimensions={0} | all-to-all | bytes 1048576 | tf_op jit(solution)/shard_map/all_to_all | solution.py:297
  112.8 5.5 margins.13
  118.6 2.4 collective-permute-start.7
  123.6 1.2 terms.13
  124.8 16.7 %all_to_all.118.refs_0_ = bf16[32,16,512]{2,1,0:T(8,128)(2,1)S(1)} all-to-all(bf16[32,16,512]{2,1,0:T(8,128)(2,1)S(1)} %terms.13), channel_id=1, replica_groups=mesh['rows'=32,'feat'=4] {'rows'}, dimensions={0} | all-to-all | bytes 1048576 | tf_op jit(solution)/shard_map/all_to_all | solution.py:297
  141.7 15.0 %all_to_all.119.coef_ref = bf16[32,16,512]{2,1,0:T(8,128)(2,1)S(1)} all-to-all(bf16[32,16,512]{2,1,0:T(8,128)(2,1)S(1)} %get-tuple-element.79), channel_id=1, replica_groups=mesh['rows'=32,'feat'=4] {'rows'}, dimensions={0} | all-to-all | bytes 1048576 | tf_op jit(solution)/shard_map/all_to_all | solution.py:297
  156.7 5.5 margins.14
  163.0 2.4 collective-permute-start.10
  169.2 16.7 %all_to_all.120.refs_0_ = bf16[32,16,512]{2,1,0:T(8,128)(2,1)S(1)} all-to-all(bf16[32,16,512]{2,1,0:T(8,128)(2,1)S(1)} %terms.14), channel_id=1, replica_groups=mesh['rows'=32,'feat'=4] {'rows'}, dimensions={0} | all-to-all | bytes 1048576 | tf_op jit(solution)/shard_map/all_to_all | solution.py:297
  186.1 15.0 %all_to_all.121.coef_ref = bf16[32,16,512]{2,1,0:T(8,128)(2,1)S(1)} all-to-all(bf16[32,16,512]{2,1,0:T(8,128)(2,1)S(1)} %get-tuple-element.84), channel_id=1, replica_groups=mesh['rows'=32,'feat'=4] {'rows'}, dimensions={0} | all-to-all | bytes 1048576 | tf_op jit(solution)/shard_map/all_to_all | solution.py:297
  201.1 5.5 margins.15
  207.0 2.4 collective-permute-start.13
  213.2 16.7 %all_to_all.122.refs_0_ = bf16[32,16,512]{2,1,0:T(8,128)(2,1)S(1)} all-to-all(bf16[32,16,512]{2,1,0:T(8,128)(2,1)S(1)} %terms.15), channel_id=1, replica_groups=mesh['rows'=32,'feat'=4] {'rows'}, dimensions={0} | all-to-all | bytes 1048576 | tf_op jit(solution)/shard_map/all_to_all | solution.py:297
  230.7 15.0 %all_to_all.123.coef_ref = bf16[32,16,512]{2,1,0:T(8,128)(2,1)S(1)} all-to-all(bf16[32,16,512]{2,1,0:T(8,128)(2,1)S(1)} %get-tuple-element.89), channel_id=1, replica_groups=mesh['rows'=32,'feat'=4] {'rows'}, dimensions={0} | all-to-all | bytes 1048576 | tf_op jit(solution)/shard_map/all_to_all | solution.py:297
  245.7 5.5 margins.16
  252.0 2.4 collective-permute-start.16
  257.1 2.0 terms.16
  259.1 5.3 all-to-all-start.10
  264.5 11.5 %all-to-all-done.10.refs_0_ = bf16[32,16,512]{2,1,0:T(8,128)(2,1)S(1)} async-done(((bf16[32,16,512]{2,1,0:T(8,128)(2,1)}), bf16[32,16,512]{2,1,0:T(8,128)(2,1)S(1)}, u32[]{:S(2)}, u32[]{:S(2)}) %all-to-all-start.10) | async-done | bytes 524320 | tf_op jit(solution)/shard_map/all_to_all | solution.py:297
  276.3 15.0 %all_to_all.124.coef_ref = bf16[32,16,512]{2,1,0:T(8,128)(2,1)S(1)} all-to-all(bf16[32,16,512]{2,1,0:T(8,128)(2,1)S(1)} %get-tuple-element.95), channel_id=1, replica_groups=mesh['rows'=32,'feat'=4] {'rows'}, dimensions={0} | all-to-all | bytes 1048576 | tf_op jit(solution)/shard_map/all_to_all | solution.py:297
  291.3 3.4 copy-done.4
  294.7 5.5 margins.17
  300.4 2.4 collective-permute-start.19
  305.6 1.2 terms.17
  306.8 16.9 %all_to_all.125.refs_0_ = bf16[32,16,512]{2,1,0:T(8,128)(2,1)S(1)} all-to-all(bf16[32,16,512]{2,1,0:T(8,128)(2,1)S(1)} %terms.17), channel_id=1, replica_groups=mesh['rows'=32,'feat'=4] {'rows'}, dimensions={0} | all-to-all | bytes 1048576 | tf_op jit(solution)/shard_map/all_to_all | solution.py:297
  323.8 15.0 %all_to_all.126.coef_ref = bf16[32,16,512]{2,1,0:T(8,128)(2,1)S(1)} all-to-all(bf16[32,16,512]{2,1,0:T(8,128)(2,1)S(1)} %get-tuple-element.100), channel_id=1, replica_groups=mesh['rows'=32,'feat'=4] {'rows'}, dimensions={0} | all-to-all | bytes 1048576 | tf_op jit(solution)/shard_map/all_to_all | solution.py:297
  338.9 5.5 margins.18
  345.2 2.4 collective-permute-start.22
  350.2 1.2 terms.18
  351.4 16.7 %all_to_all.127.refs_0_ = bf16[32,16,512]{2,1,0:T(8,128)(2,1)S(1)} all-to-all(bf16[32,16,512]{2,1,0:T(8,128)(2,1)S(1)} %terms.18), channel_id=1, replica_groups=mesh['rows'=32,'feat'=4] {'rows'}, dimensions={0} | all-to-all | bytes 1048576 | tf_op jit(solution)/shard_map/all_to_all | solution.py:297
  368.3 15.0 %all_to_all.128.coef_ref = bf16[32,16,512]{2,1,0:T(8,128)(2,1)S(1)} all-to-all(bf16[32,16,512]{2,1,0:T(8,128)(2,1)S(1)} %get-tuple-element.105), channel_id=1, replica_groups=mesh['rows'=32,'feat'=4] {'rows'}, dimensions={0} | all-to-all | bytes 1048576 | tf_op jit(solution)/shard_map/all_to_all | solution.py:297
  383.3 5.5 margins.19
  389.0 2.2 collective-permute-start.25
  395.1 16.7 %all_to_all.129.refs_0_ = bf16[32,16,512]{2,1,0:T(8,128)(2,1)S(1)} all-to-all(bf16[32,16,512]{2,1,0:T(8,128)(2,1)S(1)} %terms.19), channel_id=1, replica_groups=mesh['rows'=32,'feat'=4] {'rows'}, dimensions={0} | all-to-all | bytes 1048576 | tf_op jit(solution)/shard_map/all_to_all | solution.py:297
  411.9 15.0 %all_to_all.130.coef_ref = bf16[32,16,512]{2,1,0:T(8,128)(2,1)S(1)} all-to-all(bf16[32,16,512]{2,1,0:T(8,128)(2,1)S(1)} %get-tuple-element.110), channel_id=1, replica_groups=mesh['rows'=32,'feat'=4] {'rows'}, dimensions={0} | all-to-all | bytes 1048576 | tf_op jit(solution)/shard_map/all_to_all | solution.py:297
  426.9 5.5 margins.20
  433.4 2.4 collective-permute-start.28
  439.7 16.7 %all_to_all.131.refs_0_ = bf16[32,16,512]{2,1,0:T(8,128)(2,1)S(1)} all-to-all(bf16[32,16,512]{2,1,0:T(8,128)(2,1)S(1)} %terms.20), channel_id=1, replica_groups=mesh['rows'=32,'feat'=4] {'rows'}, dimensions={0} | all-to-all | bytes 1048576 | tf_op jit(solution)/shard_map/all_to_all | solution.py:297
  457.4 1.4 copy-done.7
  458.7 16.3 %all_to_all.132.coef_ref = bf16[32,16,640]{2,1,0:T(8,128)(2,1)S(1)} all-to-all(bf16[32,16,640]{2,1,0:T(8,128)(2,1)S(1)} %get-tuple-element.118), channel_id=1, replica_groups=mesh['rows'=32,'feat'=4] {'rows'}, dimensions={0} | all-to-all | bytes 1310720 | tf_op jit(solution)/shard_map/all_to_all | solution.py:297
  475.1 5.6 %margins.21 = (f32[16,384]{1,0:T(8,128)S(1)}, bf16[256,16384]{1,0:T(8,128)(2,1)S(1)}) custom-call(bf16[32,16,640]{2,1,0:T(8,128)(2,1)S(1)} %all_to_all.132.coef_ref, bf16[256,16384]{1,0:T(8,128)(2,1)S(1)} %bitcast.19), custom_call_target="tpu_custom_call" | custom-call | flops 134217728 | bytes 8388608 | tf_op jit(solution)/shard_map/margins/pallas_call | solution.py:85
  480.7 2.4 collective-permute-start.31
  486.0 1.2 terms.21
  487.2 17.9 %all_to_all.133.refs_0_ = bf16[32,16,640]{2,1,0:T(8,128)(2,1)S(1)} all-to-all(bf16[32,16,640]{2,1,0:T(8,128)(2,1)S(1)} %get-tuple-element.124), channel_id=1, replica_groups=mesh['rows'=32,'feat'=4] {'rows'}, dimensions={0} | all-to-all | bytes 1310720 | tf_op jit(solution)/shard_map/all_to_all | solution.py:297
  505.2 15.1 %all_to_all.134.arrived_ref = bf16[32,16,512]{2,1,0:T(8,128)(2,1)S(1)} all-to-all(bf16[32,16,512]{2,1,0:T(8,128)(2,1)S(1)} %get-tuple-element.125), channel_id=1, replica_groups=mesh['rows'=32,'feat'=4] {'rows'}, dimensions={0} | all-to-all | bytes 1048576 | tf_op jit(solution)/shard_map/all_to_all | solution.py:297
  520.3 4.5 all-to-all-start.20
  526.3 26.6 %all-to-all-done.20.ends_ref = f32[32,32,512]{2,1,0:T(8,128)} async-done(((f32[32,32,512]{2,1,0:T(8,128)}), f32[32,32,512]{2,1,0:T(8,128)}, u32[]{:S(2)}, u32[]{:S(2)}) %all-to-all-start.20) | async-done | bytes 2097184 | tf_op jit(solution)/shard_map/all_to_all | solution.py:297
  553.0 3.8 finish.1
  (130 shorter events, 43.8 us)
Async XLA Ops:
  0.6 20.2 %copy-start = (f32[8,4,16384]{2,1,0:T(4,128)S(1)}, f32[8,4,16384]{2,1,0:T(4,128)}, u32[]{:S(2)}) copy-start(f32[8,4,16384]{2,1,0:T(4,128)} %param.10) | copy-start | bytes 6291460
  0.6 3.5 copy-start.2
  4.2 1.2 copy-start.8
  5.4 15.5 %copy-start.12 = (s32[8]{0:T(128)S(1)}, s32[8]{0:T(128)}, u32[]{:S(2)}) copy-start(s32[8]{0:T(128)} %param.11) | copy-start | bytes 100
  5.4 15.5 %copy-start.9 = (s32[256]{0:T(256)S(1)}, s32[256]{0:T(256)}, u32[]{:S(2)}) copy-start(s32[256]{0:T(256)} %param.8) | copy-start | bytes 3076
  5.4 32.4 %copy-start.11 = (f32[8]{0:T(128)S(1)}, f32[8]{0:T(128)}, u32[]{:S(2)}) copy-start(f32[8]{0:T(128)} %param.13) | copy-start | bytes 100
  11.0 3.3 copy-start.5
  14.4 6.6 %collective-permute-start = (f32[16,256]{1,0:T(8,128)S(1)}, f32[16,256]{1,0:T(8,128)S(1)}, u32[]{:S(2)}, u32[]{:S(2)}) collective-permute-start(f32[16,256]{1,0:T(8,128)S(1)} %get-tuple-element.67.refs_0_), channel_id=1, source_target_pairs={{0,1},{1,2},{2,3},{3,0},{4,5},{5,6},{6,7},{7,4},{8,9},{9,10},{10,1... | collective-permute-start | bytes 49160 | tf_op jit(solution)/shard_map/ppermute | solution.py:301
  16.8 4.6 collective-permute-start.1
  20.1 2.7 collective-permute-start.2
  22.9 3.4 copy-start.6
  28.2 20.9 %all-to-all-start = ((bf16[32,16,512]{2,1,0:T(8,128)(2,1)}), bf16[32,16,512]{2,1,0:T(8,128)(2,1)S(1)}, u32[]{:S(2)}, u32[]{:S(2)}) async-start(bf16[32,16,512]{2,1,0:T(8,128)(2,1)} %terms.11), calls=%async_computation | async-start | bytes 1048576 | tf_op jit(solution)/shard_map/all_to_all | solution.py:297
  64.4 3.4 copy-start.3
  67.8 45.0 %slice-start = ((s8[8388608]{0:T(1024)(128)(4,1)}), s8[4194304]{0:T(1024)(128)(4,1)S(1)}, s32[]{:S(2)}) async-start(s8[8388608]{0:T(1024)(128)(4,1)} %bitcast.16), calls=%async_computation.23 | async-start | bytes 8388608
  73.4 3.9 collective-permute-start.3
  73.4 4.6 collective-permute-start.4
  76.5 2.6 collective-permute-start.5
  79.1 33.7 %slice-start.1 = ((s8[8388608]{0:T(1024)(128)(4,1)}), s8[4194304]{0:T(1024)(128)(4,1)S(1)}, s32[]{:S(2)}) async-start(s8[8388608]{0:T(1024)(128)(4,1)} %bitcast.16), calls=%async_computation.24 | async-start | bytes 8388608
  118.4 3.9 collective-permute-start.6
  118.6 4.1 collective-permute-start.7
  121.0 2.6 collective-permute-start.8
  162.2 3.9 collective-permute-start.9
  163.0 4.1 collective-permute-start.10
  165.4 2.6 collective-permute-start.11
  206.6 4.0 collective-permute-start.12
  207.0 4.1 collective-permute-start.13
  209.5 2.6 collective-permute-start.14
  245.7 18.8 %copy-start.10 = (s32[2,16]{1,0:T(2,128)S(1)}, s32[2,16]{1,0:T(2,128)}, u32[]{:S(2)}) copy-start(s32[2,16]{1,0:T(2,128)} %param.12) | copy-start | bytes 388
  251.3 3.9 collective-permute-start.15
  252.0 4.1 collective-permute-start.16
  254.5 2.6 collective-permute-start.17
  259.1 16.9 %all-to-all-start.10 = ((bf16[32,16,512]{2,1,0:T(8,128)(2,1)}), bf16[32,16,512]{2,1,0:T(8,128)(2,1)S(1)}, u32[]{:S(2)}, u32[]{:S(2)}) async-start(bf16[32,16,512]{2,1,0:T(8,128)(2,1)} %get-tuple-element.92), calls=%async_computation.10 | async-start | bytes 1048576 | tf_op jit(solution)/shard_map/all_to_all | solution.py:297
  291.3 3.4 copy-start.4
  294.7 44.2 %slice-start.2 = ((s8[8388608]{0:T(1024)(128)(4,1)}), s8[4194304]{0:T(1024)(128)(4,1)S(1)}, s32[]{:S(2)}) async-start(s8[8388608]{0:T(1024)(128)(4,1)} %bitcast.18), calls=%async_computation.25 | async-start | bytes 8388608
  300.2 3.9 collective-permute-start.18
  300.4 4.1 collective-permute-start.19
  302.9 2.8 collective-permute-start.20
  305.6 33.2 %slice-start.3 = ((s8[8388608]{0:T(1024)(128)(4,1)}), s8[4194304]{0:T(1024)(128)(4,1)S(1)}, s32[]{:S(2)}) async-start(s8[8388608]{0:T(1024)(128)(4,1)} %bitcast.18), calls=%async_computation.26 | async-start | bytes 8388608
  344.4 3.9 collective-permute-start.21
  345.2 4.1 collective-permute-start.22
  347.6 2.6 collective-permute-start.23
  388.8 3.9 collective-permute-start.24
  389.0 4.1 collective-permute-start.25
  391.3 2.6 collective-permute-start.26
  432.5 3.9 collective-permute-start.27
  433.4 4.1 collective-permute-start.28
  435.9 2.6 collective-permute-start.29
  457.4 1.4 copy-start.7
  480.6 4.0 collective-permute-start.30
  480.7 4.4 collective-permute-start.31
  483.1 2.9 collective-permute-start.32
  486.0 70.7 %copy-start.1 = (f32[8,4,16384]{2,1,0:T(4,128)S(1)}, f32[8,4,16384]{2,1,0:T(4,128)}, u32[]{:S(2)}) copy-start(f32[8,4,16384]{2,1,0:T(4,128)} %param.10) | copy-start | bytes 6291460
  520.3 32.6 %all-to-all-start.20 = ((f32[32,32,512]{2,1,0:T(8,128)}), f32[32,32,512]{2,1,0:T(8,128)}, u32[]{:S(2)}, u32[]{:S(2)}) async-start(f32[32,32,512]{2,1,0:T(8,128)} %copy-done.7), calls=%async_computation.20 | async-start | bytes 4194304 | tf_op jit(solution)/shard_map/all_to_all | solution.py:297

commit v2 on v0

v2 whole, which is shorter than its diff:
```python
import jax
import jax.numpy as jnp
from jax import lax
from jax.experimental import pallas as pl
from jax.experimental.pallas import tpu as pltpu
from jax.sharding import PartitionSpec as P

FEATURES = 65536
TRANS = 2
LEAP = 5
PAIRS = 8
CHAINS = 16
EXTRA = 128
CHUNKS = 8
GROUP = 4

F32 = jnp.float32
BF16 = jnp.bfloat16
VMEM = pl.BlockSpec(memory_space=pltpu.VMEM)
HBM = pl.BlockSpec(memory_space=pltpu.HBM)
SMEM = pl.BlockSpec(memory_space=pltpu.SMEM)
PARAMS = pltpu.CompilerParams(vmem_limit_bytes=6 * 1024 * 1024)
CROSS = (((1,), (1,)), ((), ()))


def call(body, name, ins, outs, scratch=(), flops=0):
    return pl.pallas_call(
        body,
        in_specs=[spec for _, spec in ins],
        out_specs=[VMEM] * len(outs),
        out_shape=[jax.ShapeDtypeStruct(*o) for o in outs],
        scratch_shapes=list(scratch),
        compiler_params=PARAMS,
        cost_estimate=pl.CostEstimate(flops=flops, bytes_accessed=flops // 16, transcendentals=0),
        name=name,
    )(*[a for a, _ in ins])


def vmem(*arrays):
    return [(a, VMEM) for a in arrays]


def first_margins(start, design):
    rows, width = design.shape
    step = width // CHUNKS

    def body(start_ref, design_ref, margins_ref, held_ref, sems):
        copies = []
        for i in range(CHUNKS):
            cols = pl.ds(i * step, step)
            copies.append(
                pltpu.make_async_copy(design_ref.at[:, cols], held_ref.at[:, cols], sems.at[i])
            )
            copies[-1].start()
        total = jnp.zeros((CHAINS, rows), F32)
        for i in range(CHUNKS):
            cols = slice(i * step, (i + 1) * step)
            copies[i].wait()
            total = total + lax.dot_general(
                start_ref[:, cols].astype(BF16), held_ref[:, cols], CROSS, preferred_element_type=F32
            )
        margins_ref[...] = total

    return call(
        body,
        "margins_start",
        [(start, VMEM), (design, HBM)],
        [((CHAINS, rows), F32), (design.shape, design.dtype)],
        [pltpu.SemaphoreType.DMA((CHUNKS,))],
        2 * CHAINS * rows * width,
    )


def draw_momenta(momenta, lag_offsets):
    _, _, width = momenta.shape

    def body(lag_ref, bank_ref, *out_refs):
        for s, out_ref in enumerate(out_refs):
            for k in range(PAIRS):
                out_ref[2 * k : 2 * k + 1] = bank_ref[k, pl.ds(s + lag_ref[k], 1)]
                out_ref[2 * k + 1 : 2 * k + 2] = bank_ref[k, s : s + 1]

    return call(
        body,
        "draw",
        [(lag_offsets, SMEM), (momenta, VMEM)],
        [((CHAINS, width), F32)] * TRANS,
    )


def square_gap(position):
    gap = position - pltpu.roll(position, CHAINS - 1, 0)
    return jnp.sum(gap * gap, axis=1, keepdims=True)


def margins_kernel(mode, held, arrived, h, state):
    rows, width = held.shape
    blocks, _, block = arrived.shape
    names = list(state)
    wide = ((CHAINS, width), F32)
    outs = {"margins": ((CHAINS, rows + (EXTRA if mode == "last" else 0)), F32), "q": wide, "p": wide}
    if mode == "turn":
        outs["pos"] = wide
        outs["gap"] = ((CHAINS, EXTRA), F32)
    if mode == "last":
        outs["pos"] = wide

    def body(held_ref, arrived_ref, h_ref, *refs):
        ins = dict(zip(names, refs))
        out = dict(zip(outs, refs[len(names) :]))
        h_col = h_ref[...]
        h_wide = jnp.broadcast_to(h_col[:, :1], (CHAINS, block))
        total = jnp.zeros((CHAINS, rows), F32)
        gap = jnp.zeros((CHAINS, 1), F32)
        if mode in ("turn", "last"):
            keep = jnp.broadcast_to(ins["keep"][:, :1], (CHAINS, block)) != 0.0
        for b in range(blocks):
            cols = slice(b * block, (b + 1) * block)
            g = arrived_ref[b].astype(F32)
            q = ins["q"][:, cols]
            if mode == "first":
                p = ins["mom"][:, cols] + 0.5 * h_wide * (g - q)
            elif mode == "turn":
                q0 = ins["q0"][:, cols]
                pos = jnp.where(keep, q, q0)
                gradient = jnp.where(keep, g - q, ins["g0"][b].astype(F32) - q0)
                p = ins["mom"][:, cols] + 0.5 * h_wide * gradient
                q = pos
                out["pos"][:, cols] = pos
                gap = gap + square_gap(pos)
            else:
                p = ins["p"][:, cols] + h_wide * (g - q)
            q = q + h_wide * p
            out["p"][:, cols] = p
            out["q"][:, cols] = q
            if mode == "last":
                pos = jnp.where(keep, q, ins["pos"][:, cols])
                out["pos"][:, cols] = pos
                gap = gap + square_gap(pos)
            total = total + lax.dot_general(
                q.astype(BF16), held_ref[:, cols], CROSS, preferred_element_type=F32
            )
        if mode == "turn":
            out["gap"][...] = jnp.broadcast_to(gap, (CHAINS, EXTRA))
        if mode == "last":
            lanes = lax.broadcasted_iota(jnp.int32, (CHAINS, EXTRA), 1)
            out["margins"][:, rows:] = jnp.where(lanes == 0, ins["gap"][...], gap)
        out["margins"][:, :rows] = total

    result = call(
        body,
        "margins_" + mode,
        vmem(held, arrived, h, *state.values()),
        list(outs.values()),
        flops=2 * CHAINS * rows * width,
    )
    return dict(zip(outs, result))


def split3(column, first_lane):
    lanes = lax.broadcasted_iota(jnp.int32, (CHAINS, EXTRA), 1) - first_lane
    high = column.astype(BF16).astype(F32)
    middle = (column - high).astype(BF16).astype(F32)
    low = column - high - middle
    out = jnp.where(lanes == 0, high, jnp.zeros((CHAINS, EXTRA), F32))
    out = jnp.where(lanes == 1, middle, out)
    return jnp.where(lanes == 2, low, out)


def terms_kernel(partials, signs, held, blocks, likes, earlier):
    rows, width = held.shape
    block = width // blocks
    extended = earlier is not None

    def body(*refs):
        own, one, two, three, sign_ref, held_ref = refs[:6]
        rest = list(refs[6:])
        earlier_ref = rest.pop(0) if extended else None
        out_ref = rest.pop(0)
        total = (own[...] + two[...]) + (one[...] + three[...])
        sign = sign_ref[...]
        signed = sign * total[:, :rows]
        weights = (sign * jax.nn.sigmoid(-signed)).astype(BF16)
        if likes:
            terms = jnp.minimum(signed, 0.0) - jnp.log1p(jnp.exp(-jnp.abs(signed)))
            like = jnp.sum(terms, axis=1, keepdims=True)
            if extended:
                side = split3(earlier_ref[...][:, :1], 0) + split3(like, 3)
                side = side.astype(BF16)
                for b in range(blocks):
                    out_ref[b, :, block:] = side
                rest[0][...] = total[:, rows:]
            else:
                rest[0][...] = jnp.broadcast_to(like, (CHAINS, EXTRA))
        for b in range(0, blocks, GROUP):
            terms = jnp.dot(
                weights,
                held_ref[:, b * block : (b + GROUP) * block],
                preferred_element_type=F32,
            ).astype(BF16)
            for j in range(GROUP):
                out_ref[b + j, :, :block] = terms[:, j * block : (j + 1) * block]

    outs = [((blocks, CHAINS, block + (EXTRA if extended else 0)), BF16)]
    if likes:
        outs.append(((CHAINS, EXTRA), F32))
    return call(
        body,
        "terms",
        vmem(*partials, signs, held, *([earlier] if extended else [])),
        outs,
        flops=2 * CHAINS * rows * width,
    )


def sum_kernel(arrived, residual, block, likes):
    blocks = arrived.shape[0]
    carried = residual is not None

    def body(*refs):
        arrived_ref = refs[0]
        send_ref, residual_ref = refs[2 if carried else 1 :][:2]
        parts = [arrived_ref[b, :, :block].astype(F32) for b in range(blocks)]
        while len(parts) > 1:
            parts = [parts[i] + parts[i + 1] for i in range(0, len(parts), 2)]
        exact = parts[0] + refs[1][...] if carried else parts[0]
        send = exact.astype(BF16)
        residual_ref[...] = exact - send.astype(F32)
        for b in range(blocks):
            send_ref[b] = send
        if likes:
            side = jnp.zeros((CHAINS, EXTRA), F32)
            for b in range(blocks):
                side = side + arrived_ref[b, :, block:].astype(F32)
            refs[-1][...] = side

    outs = [((blocks, CHAINS, block), BF16), ((CHAINS, block), F32)]
    if likes:
        outs.append(((CHAINS, EXTRA), F32))
    return call(body, "sum", vmem(arrived, *([residual] if carried else [])), outs)


def finish_kernel(arrived, h, p, q):
    blocks, _, block = arrived.shape

    def body(arrived_ref, h_ref, p_ref, q_ref, out_ref):
        half = 0.5 * jnp.broadcast_to(h_ref[...][:, :1], (CHAINS, block))
        for b in range(blocks):
            cols = slice(b * block, (b + 1) * block)
            out_ref[:, cols] = p_ref[:, cols] + half * (arrived_ref[b].astype(F32) - q_ref[:, cols])

    return call(body, "finish", vmem(arrived, h, p, q), [((CHAINS, blocks * block), F32)])[0]


def on_device(design, labels, start_position, momenta, lag_offsets, accept_bits, step_sizes):
    rows, width = design.shape
    blocks = lax.axis_size("rows")
    ring = lax.axis_size("feat")
    block = width // blocks
    signs = labels.astype(F32)[None, :]
    h = jnp.broadcast_to(jnp.repeat(step_sizes, 2)[:, None], (CHAINS, EXTRA))
    keeps = [
        jnp.broadcast_to(accept_bits[s].astype(F32)[:, None], (CHAINS, EXTRA)) for s in range(TRANS)
    ]
    moms = draw_momenta(momenta, lag_offsets)
    design, start, signs, h, keeps, moms = lax.optimization_barrier(
        (design, start_position, signs, h, keeps, moms)
    )

    def exchange(blocked):
        return lax.all_to_all(blocked, "rows", 0, 0)

    def around(margins):
        return [margins] + [
            lax.ppermute(margins, "feat", [(i, (i + k) % ring) for i in range(ring)])
            for k in range(1, ring)
        ]

    def gradient(margins, residual, likes=False, earlier=None):
        out, *side = terms_kernel(around(margins), signs, held, blocks, likes, earlier)
        send, residual, *totals = sum_kernel(exchange(out), residual, block, earlier is not None)
        return exchange(send), residual, side + totals

    margins, held = first_margins(start, design)
    g0, residual, _ = gradient(margins, None)
    g = g0
    now = {"q": start}
    for leap in range(LEAP):
        if leap == 0:
            now = margins_kernel("first", held, g, h, {"q": start, "mom": moms[0]})
        else:
            now = margins_kernel("mid", held, g, h, {"q": now["q"], "p": now["p"]})
        g, residual, side = gradient(now["margins"], residual, likes=leap + 1 == LEAP)
    (like,) = side
    for leap in range(LEAP):
        if leap == 0:
            state = {"q": now["q"], "q0": start, "g0": g0, "mom": moms[1], "keep": keeps[0]}
            now = margins_kernel("turn", held, g, h, state)
            position, gap = now["pos"], now["gap"]
        elif leap + 1 < LEAP:
            now = margins_kernel("mid", held, g, h, {"q": now["q"], "p": now["p"]})
        else:
            state = {"q": now["q"], "p": now["p"], "pos": position, "gap": gap, "keep": keeps[1]}
            now = margins_kernel("last", held, g, h, state)
        last = leap + 1 == LEAP
        g, residual, side = gradient(now["margins"], residual, last, like if last else None)
    gaps, likes = side
    momentum = finish_kernel(g, h, now["p"], now["q"])
    likes = likes[:, :6].reshape(CHAINS, 2, 3).sum(2).T
    squares = gaps[0::2, :2].T
    return (
        now["pos"],
        momentum,
        likes / (rows * blocks),
        jnp.sqrt(squares / FEATURES + 1e-06),
    )


def solution(mesh):
    return jax.shard_map(
        on_device,
        mesh=mesh,
        in_specs=(
            P("rows", "feat"),
            P("rows"),
            P(None, "feat"),
            P(None, None, "feat"),
            P(),
            P(),
            P(),
        ),
        out_specs=(P(None, "feat"), P(None, "feat"), P(), P()),
        check_vma=False,
    )
```

time: 1520 us -> 485 us (0.32)
  waiting for transfers between devices: 1030 us -> 50.6 us
  matrix products: 125 us -> 0 us
  blocking collectives: 278 us -> 337 us
  Pallas kernels: 0 us -> 47.7 us
  other arithmetic: 32.4 us -> 2.04 us
  starting transfers between devices: 1.94 us -> 30.1 us
  local copies, waits for them, and re-layouts: 27.8 us -> 8.62 us
    psum x11 -> x0, waiting for transfers between devices: 1030 us -> none  [gradient_at(): summed = lax.psum(row_terms, 'rows')]
    all_to_all x0 -> x21, blocking collectives: none -> 337 us  [exchange(): return lax.all_to_all(blocked, 'rows', 0, 0)]
    psum x13 -> x0, blocking collectives: 278 us -> none  [the longest x11 149 us: gradient_at(): margins = lax.psum(partial_margins, 'feat')]
    dot_general x22 -> x0, matrix products: 125 us -> none  [the longest x11 63.6 us: gradient_at(): lax.dot_general(rounded, design, (((1,), (1,)), ((), ())), preferred_elem...]
    pallas_call x0 -> x35, Pallas kernels: none -> 47.7 us  [call(): pl.pallas_call(body, in_specs=[spec for _, spec in ins], out_specs=[VMEM]...]
    ppermute x0 -> x33, waiting for transfers between devices: none -> 40.3 us  [around(): lax.ppermute(margins, 'feat', [(i, (i + k) % ring) for i in range(ring)])]
    ppermute x0 -> x33, starting transfers between devices: none -> 26.4 us  [around(): lax.ppermute(margins, 'feat', [(i, (i + k) % ring) for i in range(ring)])]
  transfers between devices with their start and end apart: 11 -> 34, of which waited for: 10 -> 32; matrix products, arithmetic and copies ran while one was open for 2% -> 0% of each run, Pallas kernels for 0% -> 0%
where the time goes in v2:
time: 485 us; the launch traced here: 477 us
  blocking collectives  337 us (69%)
  waiting for transfers between devices  50.6 us (10%)
  Pallas kernels  47.7 us (10%)
  starting transfers between devices  30.1 us (6%)
  local copies, waits for them, and re-layouts  8.62 us (2%)
    all_to_all x21, blocking collectives, exchange(): return lax.all_to_all(blocked, 'rows', 0, 0)  337 us
    pallas_call x35, Pallas kernels, call(): pl.pallas_call(body, in_specs=[spec for _, spec in ins], out_specs=[VMEM]...  47.7 us
    ppermute x33, waiting for transfers between devices, around(): lax.ppermute(margins, 'feat', [(i, (i + k) % ring) for i in range(ring)])  40.3 us
    ppermute x33, starting transfers between devices, around(): lax.ppermute(margins, 'feat', [(i, (i + k) % ring) for i in range(ring)])  26.4 us
    all_to_all x1, waiting for transfers between devices, exchange(): return lax.all_to_all(blocked, 'rows', 0, 0)  10.2 us
  transfers between devices with their start and end apart: 34, of which 32 were waited for; matrix products, arithmetic and copies ran while one was open for 0% of the time, Pallas kernels for 0%

profile of v2, /device:TPU:1, one launch (start us, length us, event | category | flops | bytes accessed | tf_op | source)
XLA Modules:
  0.0 477.1 jit_solution(6626573534535426299)
XLA Ops:
  2.9 1.6 copy-done.3
  6.4 1.2 copy-done
  7.6 3.4 copy-done.2
  11.0 5.3 %margins_start.1 = (f32[16,256]{1,0:T(8,128)S(1)}, bf16[256,16384]{1,0:T(8,128)(2,1)S(1)}) custom-call(f32[16,16384]{1,0:T(8,128)S(1)} %copy-done, bf16[256,16384]{1,0:T(8,128)(2,1)S(1)} %copy-done.2), custom_call_target="tpu_custom_call" | custom-call | flops 134217728 | bytes 8388608 | tf_op jit(solution)/shard_map/margins_start/pallas_call | solution.py:27
  16.3 4.6 collective-permute-start.2
  21.8 3.2 collective-permute-done.1.refs_2_
  25.0 1.2 terms.11
  26.2 20.6 %all_to_all.110.refs_0_ = bf16[32,16,512]{2,1,0:T(8,128)(2,1)S(1)} all-to-all(bf16[32,16,512]{2,1,0:T(8,128)(2,1)S(1)} %terms.11), channel_id=1, replica_groups=mesh['rows'=32,'feat'=4] {'rows'}, dimensions={0} | all-to-all | bytes 1048576 | tf_op jit(solution)/shard_map/all_to_all | solution.py:271
  47.0 15.0 %all_to_all.111.arrived_ref.refs_2_ = bf16[32,16,512]{2,1,0:T(8,128)(2,1)S(1)} all-to-all(bf16[32,16,512]{2,1,0:T(8,128)(2,1)S(1)} %get-tuple-element.81), channel_id=1, replica_groups=mesh['rows'=32,'feat'=4] {'rows'}, dimensions={0} | all-to-all | bytes 1048576 | tf_op jit(solution)/shard_map/all_to_all | solution.py:271
  62.0 2.4 margins_first.1
  64.8 1.3 collective-permute-start.4
  67.0 1.9 collective-permute-done.4.refs_2_
  70.0 1.2 terms.12
  71.2 16.5 %all_to_all.112.refs_0_ = bf16[32,16,512]{2,1,0:T(8,128)(2,1)S(1)} all-to-all(bf16[32,16,512]{2,1,0:T(8,128)(2,1)S(1)} %terms.12), channel_id=1, replica_groups=mesh['rows'=32,'feat'=4] {'rows'}, dimensions={0} | all-to-all | bytes 1048576 | tf_op jit(solution)/shard_map/all_to_all | solution.py:271
  87.7 15.5 %all_to_all.113.arrived_ref = bf16[32,16,512]{2,1,0:T(8,128)(2,1)S(1)} all-to-all(bf16[32,16,512]{2,1,0:T(8,128)(2,1)S(1)} %get-tuple-element.86), channel_id=1, replica_groups=mesh['rows'=32,'feat'=4] {'rows'}, dimensions={0} | all-to-all | bytes 1048576 | tf_op jit(solution)/shard_map/all_to_all | solution.py:271
  103.2 2.3 margins_mid.7
  108.2 2.6 collective-permute-done.7.refs_2_
  111.4 1.2 terms.13
  112.6 16.4 %all_to_all.114.refs_0_ = bf16[32,16,512]{2,1,0:T(8,128)(2,1)S(1)} all-to-all(bf16[32,16,512]{2,1,0:T(8,128)(2,1)S(1)} %terms.13), channel_id=1, replica_groups=mesh['rows'=32,'feat'=4] {'rows'}, dimensions={0} | all-to-all | bytes 1048576 | tf_op jit(solution)/shard_map/all_to_all | solution.py:271
  129.2 15.0 %all_to_all.115.arrived_ref = bf16[32,16,512]{2,1,0:T(8,128)(2,1)S(1)} all-to-all(bf16[32,16,512]{2,1,0:T(8,128)(2,1)S(1)} %get-tuple-element.91), channel_id=1, replica_groups=mesh['rows'=32,'feat'=4] {'rows'}, dimensions={0} | all-to-all | bytes 1048576 | tf_op jit(solution)/shard_map/all_to_all | solution.py:271
  144.2 2.3 margins_mid.8
  149.1 2.4 collective-permute-done.10.refs_2_
  152.2 1.2 terms.14
  153.4 16.4 %all_to_all.116.refs_0_ = bf16[32,16,512]{2,1,0:T(8,128)(2,1)S(1)} all-to-all(bf16[32,16,512]{2,1,0:T(8,128)(2,1)S(1)} %terms.14), channel_id=1, replica_groups=mesh['rows'=32,'feat'=4] {'rows'}, dimensions={0} | all-to-all | bytes 1048576 | tf_op jit(solution)/shard_map/all_to_all | solution.py:271
  169.9 15.0 %all_to_all.117.arrived_ref = bf16[32,16,512]{2,1,0:T(8,128)(2,1)S(1)} all-to-all(bf16[32,16,512]{2,1,0:T(8,128)(2,1)S(1)} %get-tuple-element.96), channel_id=1, replica_groups=mesh['rows'=32,'feat'=4] {'rows'}, dimensions={0} | all-to-all | bytes 1048576 | tf_op jit(solution)/shard_map/all_to_all | solution.py:271
  184.9 2.4 margins_mid.9
  189.9 2.6 collective-permute-done.13.refs_2_
  193.3 1.2 terms.15
  194.5 16.5 %all_to_all.118.refs_0_ = bf16[32,16,512]{2,1,0:T(8,128)(2,1)S(1)} all-to-all(bf16[32,16,512]{2,1,0:T(8,128)(2,1)S(1)} %terms.15), channel_id=1, replica_groups=mesh['rows'=32,'feat'=4] {'rows'}, dimensions={0} | all-to-all | bytes 1048576 | tf_op jit(solution)/shard_map/all_to_all | solution.py:271
  211.1 15.0 %all_to_all.119.arrived_ref = bf16[32,16,512]{2,1,0:T(8,128)(2,1)S(1)} all-to-all(bf16[32,16,512]{2,1,0:T(8,128)(2,1)S(1)} %get-tuple-element.101), channel_id=1, replica_groups=mesh['rows'=32,'feat'=4] {'rows'}, dimensions={0} | all-to-all | bytes 1048576 | tf_op jit(solution)/shard_map/all_to_all | solution.py:271
  226.1 3.2 margins_mid.10
  231.9 2.4 collective-permute-done.16.refs_2_
  234.7 1.2 terms.16
  235.9 16.4 %all_to_all.120.refs_0_ = bf16[32,16,512]{2,1,0:T(8,128)(2,1)S(1)} all-to-all(bf16[32,16,512]{2,1,0:T(8,128)(2,1)S(1)} %get-tuple-element.105), channel_id=1, replica_groups=mesh['rows'=32,'feat'=4] {'rows'}, dimensions={0} | all-to-all | bytes 1048576 | tf_op jit(solution)/shard_map/all_to_all | solution.py:271
  252.5 15.0 %all_to_all.121.arrived_ref = bf16[32,16,512]{2,1,0:T(8,128)(2,1)S(1)} all-to-all(bf16[32,16,512]{2,1,0:T(8,128)(2,1)S(1)} %get-tuple-element.107), channel_id=1, replica_groups=mesh['rows'=32,'feat'=4] {'rows'}, dimensions={0} | all-to-all | bytes 1048576 | tf_op jit(solution)/shard_map/all_to_all | solution.py:271
  267.5 2.7 margins_turn.1
  270.2 1.3 collective-permute-start.20
  272.8 2.8 collective-permute-done.19.refs_2_
  276.2 1.2 terms.17
  277.4 16.4 %all_to_all.122.refs_0_ = bf16[32,16,512]{2,1,0:T(8,128)(2,1)S(1)} all-to-all(bf16[32,16,512]{2,1,0:T(8,128)(2,1)S(1)} %terms.17), channel_id=1, replica_groups=mesh['rows'=32,'feat'=4] {'rows'}, dimensions={0} | all-to-all | bytes 1048576 | tf_op jit(solution)/shard_map/all_to_all | solution.py:271
  294.0 15.2 %all_to_all.123.arrived_ref = bf16[32,16,512]{2,1,0:T(8,128)(2,1)S(1)} all-to-all(bf16[32,16,512]{2,1,0:T(8,128)(2,1)S(1)} %get-tuple-element.113), channel_id=1, replica_groups=mesh['rows'=32,'feat'=4] {'rows'}, dimensions={0} | all-to-all | bytes 1048576 | tf_op jit(solution)/shard_map/all_to_all | solution.py:271
  309.2 2.4 margins_mid.11
  314.2 2.2 collective-permute-done.22.refs_2_
  317.1 1.2 terms.18
  318.2 16.4 %all_to_all.124.refs_0_ = bf16[32,16,512]{2,1,0:T(8,128)(2,1)S(1)} all-to-all(bf16[32,16,512]{2,1,0:T(8,128)(2,1)S(1)} %terms.18), channel_id=1, replica_groups=mesh['rows'=32,'feat'=4] {'rows'}, dimensions={0} | all-to-all | bytes 1048576 | tf_op jit(solution)/shard_map/all_to_all | solution.py:271
  334.8 15.0 %all_to_all.125.arrived_ref = bf16[32,16,512]{2,1,0:T(8,128)(2,1)S(1)} all-to-all(bf16[32,16,512]{2,1,0:T(8,128)(2,1)S(1)} %get-tuple-element.118), channel_id=1, replica_groups=mesh['rows'=32,'feat'=4] {'rows'}, dimensions={0} | all-to-all | bytes 1048576 | tf_op jit(solution)/shard_map/all_to_all | solution.py:271
  349.8 2.3 margins_mid.12
  352.2 1.3 collective-permute-start.26
  354.8 2.8 collective-permute-done.25.refs_2_
  358.2 1.2 terms.19
  359.4 16.4 %all_to_all.126.refs_0_ = bf16[32,16,512]{2,1,0:T(8,128)(2,1)S(1)} all-to-all(bf16[32,16,512]{2,1,0:T(8,128)(2,1)S(1)} %terms.19), channel_id=1, replica_groups=mesh['rows'=32,'feat'=4] {'rows'}, dimensions={0} | all-to-all | bytes 1048576 | tf_op jit(solution)/shard_map/all_to_all | solution.py:271
  375.9 15.0 %all_to_all.127.arrived_ref = bf16[32,16,512]{2,1,0:T(8,128)(2,1)S(1)} all-to-all(bf16[32,16,512]{2,1,0:T(8,128)(2,1)S(1)} %get-tuple-element.123), channel_id=1, replica_groups=mesh['rows'=32,'feat'=4] {'rows'}, dimensions={0} | all-to-all | bytes 1048576 | tf_op jit(solution)/shard_map/all_to_all | solution.py:271
  391.0 2.3 margins_mid.13
  395.9 2.2 collective-permute-done.28.refs_2_
  398.9 1.2 terms.20
  400.1 16.5 %all_to_all.128.refs_0_ = bf16[32,16,512]{2,1,0:T(8,128)(2,1)S(1)} all-to-all(bf16[32,16,512]{2,1,0:T(8,128)(2,1)S(1)} %terms.20), channel_id=1, replica_groups=mesh['rows'=32,'feat'=4] {'rows'}, dimensions={0} | all-to-all | bytes 1048576 | tf_op jit(solution)/shard_map/all_to_all | solution.py:271
  416.7 15.0 %all_to_all.129.arrived_ref = bf16[32,16,512]{2,1,0:T(8,128)(2,1)S(1)} all-to-all(bf16[32,16,512]{2,1,0:T(8,128)(2,1)S(1)} %get-tuple-element.128), channel_id=1, replica_groups=mesh['rows'=32,'feat'=4] {'rows'}, dimensions={0} | all-to-all | bytes 1048576 | tf_op jit(solution)/shard_map/all_to_all | solution.py:271
  431.8 2.6 margins_last.1
  434.4 1.3 collective-permute-start.32
  437.5 2.4 collective-permute-done.31.refs_2_
  440.6 1.2 terms.21
  441.8 17.4 %all_to_all.130.refs_0_ = bf16[32,16,640]{2,1,0:T(8,128)(2,1)S(1)} all-to-all(bf16[32,16,640]{2,1,0:T(8,128)(2,1)S(1)} %get-tuple-element.137), channel_id=1, replica_groups=mesh['rows'=32,'feat'=4] {'rows'}, dimensions={0} | all-to-all | bytes 1310720 | tf_op jit(solution)/shard_map/all_to_all | solution.py:271
  460.1 3.7 all-to-all-start.21
  465.2 10.2 %all-to-all-done.21.arrived_ref = bf16[32,16,512]{2,1,0:T(8,128)(2,1)S(1)} async-done(((bf16[32,16,512]{2,1,0:T(8,128)(2,1)}), bf16[32,16,512]{2,1,0:T(8,128)(2,1)S(1)}, u32[]{:S(2)}, u32[]{:S(2)}) %all-to-all-start.21) | async-done | bytes 524320 | tf_op jit(solution)/shard_map/all_to_all | solution.py:271
  (84 shorter events, 37.9 us)
Async XLA Ops:
  2.9 1.6 copy-start.3
  4.5 0.7 copy-start.4
  6.4 1.2 copy-start
  7.6 3.4 copy-start.2
  11.0 51.0 %copy-start.1 = (f32[16,16384]{1,0:T(8,128)S(1)}, f32[16,16384]{1,0:T(8,128)}, u32[]{:S(2)}) copy-start(f32[16,16384]{1,0:T(8,128)} %refs_1_) | copy-start | bytes 3145732
  16.3 5.5 %collective-permute-start.2 = (f32[16,256]{1,0:T(8,128)S(1)}, f32[16,256]{1,0:T(8,128)S(1)}, u32[]{:S(2)}, u32[]{:S(2)}) collective-permute-start(f32[16,256]{1,0:T(8,128)S(1)} %get-tuple-element.79.refs_0_), channel_id=1, source_target_pairs={{0,3},{1,0},{2,1},{3,2},{4,7},{5,4},{6,5},{7,6},{8,11},{9,8},{10,9... | collective-permute-start | bytes 49160 | tf_op jit(solution)/shard_map/ppermute | solution.py:275
  20.9 4.1 collective-permute-start.1
  21.0 4.1 collective-permute-start
  64.4 2.6 collective-permute-start.5
  64.8 4.1 collective-permute-start.4
  66.2 3.8 collective-permute-start.3
  105.5 2.6 collective-permute-start.8
  106.7 4.1 collective-permute-start.7
  107.3 4.1 collective-permute-start.6
  146.5 2.6 collective-permute-start.11
  147.5 4.1 collective-permute-start.10
  148.1 4.1 collective-permute-start.9
  187.3 2.6 collective-permute-start.14
  188.5 4.1 collective-permute-start.13
  189.1 4.2 collective-permute-start.12
  229.3 2.6 collective-permute-start.17
  230.2 4.1 collective-permute-start.16
  230.6 4.1 collective-permute-start.15
  270.2 2.6 collective-permute-start.20
  271.5 4.1 collective-permute-start.19
  272.1 4.1 collective-permute-start.18
  311.6 2.6 collective-permute-start.23
  312.3 4.1 collective-permute-start.22
  312.9 4.1 collective-permute-start.21
  352.2 2.6 collective-permute-start.26
  353.5 4.1 collective-permute-start.25
  354.1 4.1 collective-permute-start.24
  393.3 2.6 collective-permute-start.29
  394.0 4.1 collective-permute-start.28
  394.7 4.2 collective-permute-start.27
  434.4 3.1 collective-permute-start.32
  435.7 4.2 collective-permute-start.31
  436.1 4.5 collective-permute-start.30
  460.1 15.3 %all-to-all-start.21 = ((bf16[32,16,512]{2,1,0:T(8,128)(2,1)}), bf16[32,16,512]{2,1,0:T(8,128)(2,1)S(1)}, u32[]{:S(2)}, u32[]{:S(2)}) async-start(bf16[32,16,512]{2,1,0:T(8,128)(2,1)} %get-tuple-element.139), calls=%async_computation.21 | async-start | bytes 1048576 | tf_op jit(solution)/shard_map/all_to_all | solution.py:271
